TPU v7x, 256 devices: a whole 4x4x8 slice. The times are simulated.
256 devices in a mesh: grp: 4 (over x), tile: 64 (over z, y, core).
Axes of the slice: x: 4, y: 4, z: 8, core: 2. Of those that a mesh axis runs over, the one named last changes fastest.
Arguments:
- bricks: float32 [512, 128, 512], P(('grp', 'tile')), may hold values from 0 to 1
- colour_table: float32 [3, 256], replicated, may hold values from 0.5 to 8
- opacity_table: float32 [256], replicated, may hold values from 2e-05 to 0.005
- depth_order: int32 [4, 64], replicated, may hold values from 0 to 63, each once within a row
Outputs:
- image: float32 [4, 65536], P(None, ('grp', 'tile'))
Inputs may be any that keep to these rules, and one draw needn't show every extreme that they name: Each row of depth_order holds every number 0 .. 63 once.
All inputs are finite; a program needn't handle non-finite values.
Results may differ from a plain program's by a relative error of at most 0.0003.
Values sent between devices are 32-bit elements; how exact they have to be, the bound alone decides.
A program may use at most 64 MiB of HBM per device.

v0:
```python
import jax
import jax.numpy as jnp
from jax import lax
from jax.sharding import PartitionSpec as P


def shade_cells(values, palette):
    knot_count = palette.shape[1]
    position = values * (knot_count - 1)
    knot_pos = lax.broadcasted_iota(jnp.float32, (knot_count, 1), 0)
    weights = jnp.maximum(0.0, 1.0 - jnp.abs(position[None, :] - knot_pos))
    return jnp.dot(
        palette, weights, precision=lax.Precision.HIGHEST, preferred_element_type=jnp.float32
    )


def render(bricks, palette):
    depth_count = bricks.shape[0]
    pixels = bricks.shape[1] * bricks.shape[2]
    slices = bricks.reshape(depth_count, pixels)
    block_len = pixels // 8

    def one_slice(depth_at, carry):
        colour, transmit = carry
        values = lax.dynamic_index_in_dim(slices, depth_at, 0, keepdims=False)
        shaded = [
            shade_cells(lax.slice_in_dim(values, j * block_len, (j + 1) * block_len), palette)
            for j in range(8)
        ]
        sample = jnp.concatenate(shaded, axis=1)
        weight = transmit * sample[3]
        colour = colour + weight[None, :] * sample[:3]
        transmit = transmit * (1.0 - sample[3])
        return (colour, transmit)

    start = (jnp.zeros((3, pixels), jnp.float32), jnp.ones((pixels,), jnp.float32))
    colour, transmit = lax.fori_loop(0, depth_count, one_slice, start)
    return jnp.concatenate([colour, (1.0 - transmit)[None, :]], axis=0)


def composite(layers):
    while layers.shape[0] > 1:
        near_half = layers[0::2]
        far_half = layers[1::2]
        layers = near_half + (1.0 - near_half[:, 3:4]) * far_half
    return layers[0]


def body(bricks, colour_table, opacity_table, depth_order):
    palette = jnp.concatenate([colour_table, opacity_table[None, :]], axis=0)
    partial_value = render(bricks, palette)
    groups = lax.axis_size("grp")
    members = lax.axis_size("tile")
    pixels = partial_value.shape[1]
    sub_len = pixels // (groups * members)
    sectioned = partial_value.reshape(1, 4, groups, members, sub_len)
    layers = lax.all_to_all(sectioned, "tile", split_axis=3, concat_axis=0, tiled=True)
    layers = layers.reshape(members, 4, groups, sub_len)
    group_index = lax.axis_index("grp")
    rank_row = lax.dynamic_index_in_dim(depth_order, group_index, 0, keepdims=False)
    by_rank = jnp.argsort(rank_row)
    ordered = jnp.take(layers, by_rank, axis=0)
    own_group = composite(ordered)
    arrived = lax.all_to_all(own_group[None], "grp", split_axis=2, concat_axis=0, tiled=True)
    result = composite(arrived).reshape(4, sub_len)
    return result


def solution(mesh):
    in_specs = (P(("grp", "tile"), None, None), P(), P(), P())
    out_specs = P(None, ("grp", "tile"))
    return jax.shard_map(body, mesh=mesh, in_specs=in_specs, out_specs=out_specs, check_vma=False)
```

profile of v0, /device:TPU:8, one launch (start us, length us, event | category | flops | bytes accessed | tf_op | source)
XLA Modules:
  0.0 153.1 jit_solution(6230588998813952491)
XLA Ops:
  0.0 0.0 copy-start
  0.0 0.0 copy-start.2
  0.0 0.0 copy-start.1
  0.0 1.5 copy.10
  1.5 0.0 copy-done.2
  1.5 0.0 copy-done.1
  1.5 96.2 %while.16 = (s32[]{:T(128)}, f32[3,65536]{1,0:T(4,128)S(1)}, f32[65536]{0:T(1024)S(1)}, f32[2,65536]{1,0:T(2,128)S(1)}, f32[4,256]{1,0:T(4,128)S(1)}, /*index=5*...) while((s32[]{:T(128)}, f32[3,65536]{1,0:T(4,128)S(1)}, ...), condition=%wide.region_2.3_spmd.clone, body=%wide.region_1.2_spmd.clone.sunk | while | flops 873332736 | bytes 6062348 | solution.py:37
  1.8 0.6 dynamic-slice_multiply_fusion.9
  2.3 5.4 %fusion.147 = f32[4,65536]{1,0:T(4,128)S(1)} fusion(f32[4,256]{1,0:T(4,128)S(1)} %get-tuple-element.225, f32[8192]{0:T(1024)S(1)} %bitcast.147), kind=kOutput, calls=%fused_computation.16.clone.1 | convolution fusion | flops 109051904 | bytes 167936 | tf_op jit(solution)/shard_map/while/body/eval_jaxpr/dot_general | solution.py:12
  7.8 5.4 %fusion.148 = f32[4,65536]{1,0:T(4,128)S(1)} fusion(f32[4,65536]{1,0:T(4,128)S(1)} %fusion.147, f32[4,256]{1,0:T(4,128)S(1)} %get-tuple-element.225, f32[8192]{0:T(1024)S(1)} %bitcast.146), kind=kOutput, calls=%fused_computation.14.clone.1 | convolution fusion | flops 109051904 | bytes 167936 | tf_op jit(solution)/shard_map/while/body/eval_jaxpr/dot_general | solution.py:12
  13.2 6.0 %fusion.149 = f32[4,65536]{1,0:T(4,128)S(1)} fusion(f32[4,65536]{1,0:T(4,128)S(1)} %fusion.148, f32[4,256]{1,0:T(4,128)S(1)} %get-tuple-element.225, f32[8192]{0:T(1024)S(1)} %bitcast.145), kind=kOutput, calls=%fused_computation.12.clone.1 | convolution fusion | flops 109051904 | bytes 167936 | tf_op jit(solution)/shard_map/while/body/eval_jaxpr/dot_general | solution.py:12
  19.2 5.4 %fusion.150 = f32[4,65536]{1,0:T(4,128)S(1)} fusion(f32[4,65536]{1,0:T(4,128)S(1)} %fusion.149, f32[4,256]{1,0:T(4,128)S(1)} %get-tuple-element.225, f32[8192]{0:T(1024)S(1)} %bitcast.144), kind=kOutput, calls=%fused_computation.10.clone.1 | convolution fusion | flops 109051904 | bytes 167936 | tf_op jit(solution)/shard_map/while/body/eval_jaxpr/dot_general | solution.py:12
  24.6 5.6 %fusion.151 = f32[4,65536]{1,0:T(4,128)S(1)} fusion(f32[4,65536]{1,0:T(4,128)S(1)} %fusion.150, f32[4,256]{1,0:T(4,128)S(1)} %get-tuple-element.225, f32[8192]{0:T(1024)S(1)} %bitcast.143), kind=kOutput, calls=%fused_computation.8.clone.1 | convolution fusion | flops 109051904 | bytes 167936 | tf_op jit(solution)/shard_map/while/body/eval_jaxpr/dot_general | solution.py:12
  30.2 5.4 %fusion.152 = f32[4,65536]{1,0:T(4,128)S(1)} fusion(f32[4,65536]{1,0:T(4,128)S(1)} %fusion.151, f32[4,256]{1,0:T(4,128)S(1)} %get-tuple-element.225, f32[8192]{0:T(1024)S(1)} %bitcast.142), kind=kOutput, calls=%fused_computation.6.clone.1 | convolution fusion | flops 109051904 | bytes 167936 | tf_op jit(solution)/shard_map/while/body/eval_jaxpr/dot_general | solution.py:12
  35.7 5.7 %fusion.153 = f32[4,65536]{1,0:T(4,128)S(1)} fusion(f32[4,65536]{1,0:T(4,128)S(1)} %fusion.152, f32[4,256]{1,0:T(4,128)S(1)} %get-tuple-element.225, f32[8192]{0:T(1024)S(1)} %bitcast.141), kind=kOutput, calls=%fused_computation.4.clone.1 | convolution fusion | flops 109051904 | bytes 167936 | tf_op jit(solution)/shard_map/while/body/eval_jaxpr/dot_general | solution.py:12
  41.3 5.4 %fusion.154 = f32[4,65536]{1,0:T(4,128)S(1)} fusion(f32[4,65536]{1,0:T(4,128)S(1)} %fusion.153, f32[4,256]{1,0:T(4,128)S(1)} %get-tuple-element.225, f32[8192]{0:T(1024)S(1)} %bitcast.140), kind=kOutput, calls=%fused_computation.2.clone.1 | convolution fusion | flops 109051904 | bytes 167936 | tf_op jit(solution)/shard_map/while/body/eval_jaxpr/dot_general | solution.py:12
  46.8 0.3 slice.255
  47.1 0.2 subtract_multiply_fusion.2
  47.2 0.6 fusion.155
  48.3 0.6 dynamic-slice_multiply_fusion.9
  48.8 5.4 %fusion.147 = f32[4,65536]{1,0:T(4,128)S(1)} fusion(f32[4,256]{1,0:T(4,128)S(1)} %get-tuple-element.225, f32[8192]{0:T(1024)S(1)} %bitcast.147), kind=kOutput, calls=%fused_computation.16.clone.1 | convolution fusion | flops 109051904 | bytes 167936 | tf_op jit(solution)/shard_map/while/body/eval_jaxpr/dot_general | solution.py:12
  54.2 5.4 %fusion.148 = f32[4,65536]{1,0:T(4,128)S(1)} fusion(f32[4,65536]{1,0:T(4,128)S(1)} %fusion.147, f32[4,256]{1,0:T(4,128)S(1)} %get-tuple-element.225, f32[8192]{0:T(1024)S(1)} %bitcast.146), kind=kOutput, calls=%fused_computation.14.clone.1 | convolution fusion | flops 109051904 | bytes 167936 | tf_op jit(solution)/shard_map/while/body/eval_jaxpr/dot_general | solution.py:12
  59.7 5.6 %fusion.149 = f32[4,65536]{1,0:T(4,128)S(1)} fusion(f32[4,65536]{1,0:T(4,128)S(1)} %fusion.148, f32[4,256]{1,0:T(4,128)S(1)} %get-tuple-element.225, f32[8192]{0:T(1024)S(1)} %bitcast.145), kind=kOutput, calls=%fused_computation.12.clone.1 | convolution fusion | flops 109051904 | bytes 167936 | tf_op jit(solution)/shard_map/while/body/eval_jaxpr/dot_general | solution.py:12
  65.3 5.4 %fusion.150 = f32[4,65536]{1,0:T(4,128)S(1)} fusion(f32[4,65536]{1,0:T(4,128)S(1)} %fusion.149, f32[4,256]{1,0:T(4,128)S(1)} %get-tuple-element.225, f32[8192]{0:T(1024)S(1)} %bitcast.144), kind=kOutput, calls=%fused_computation.10.clone.1 | convolution fusion | flops 109051904 | bytes 167936 | tf_op jit(solution)/shard_map/while/body/eval_jaxpr/dot_general | solution.py:12
  70.8 5.7 %fusion.151 = f32[4,65536]{1,0:T(4,128)S(1)} fusion(f32[4,65536]{1,0:T(4,128)S(1)} %fusion.150, f32[4,256]{1,0:T(4,128)S(1)} %get-tuple-element.225, f32[8192]{0:T(1024)S(1)} %bitcast.143), kind=kOutput, calls=%fused_computation.8.clone.1 | convolution fusion | flops 109051904 | bytes 167936 | tf_op jit(solution)/shard_map/while/body/eval_jaxpr/dot_general | solution.py:12
  76.4 5.4 %fusion.152 = f32[4,65536]{1,0:T(4,128)S(1)} fusion(f32[4,65536]{1,0:T(4,128)S(1)} %fusion.151, f32[4,256]{1,0:T(4,128)S(1)} %get-tuple-element.225, f32[8192]{0:T(1024)S(1)} %bitcast.142), kind=kOutput, calls=%fused_computation.6.clone.1 | convolution fusion | flops 109051904 | bytes 167936 | tf_op jit(solution)/shard_map/while/body/eval_jaxpr/dot_general | solution.py:12
  81.9 5.8 %fusion.153 = f32[4,65536]{1,0:T(4,128)S(1)} fusion(f32[4,65536]{1,0:T(4,128)S(1)} %fusion.152, f32[4,256]{1,0:T(4,128)S(1)} %get-tuple-element.225, f32[8192]{0:T(1024)S(1)} %bitcast.141), kind=kOutput, calls=%fused_computation.4.clone.1 | convolution fusion | flops 109051904 | bytes 167936 | tf_op jit(solution)/shard_map/while/body/eval_jaxpr/dot_general | solution.py:12
  87.7 5.4 %fusion.154 = f32[4,65536]{1,0:T(4,128)S(1)} fusion(f32[4,65536]{1,0:T(4,128)S(1)} %fusion.153, f32[4,256]{1,0:T(4,128)S(1)} %get-tuple-element.225, f32[8192]{0:T(1024)S(1)} %bitcast.140), kind=kOutput, calls=%fused_computation.2.clone.1 | convolution fusion | flops 109051904 | bytes 167936 | tf_op jit(solution)/shard_map/while/body/eval_jaxpr/dot_general | solution.py:12
  93.1 0.3 slice.255
  93.4 0.2 subtract_multiply_fusion.2
  93.6 0.6 fusion.155
  97.8 0.1 concatenate.20
  97.8 0.2 copy.11
  98.0 0.1 pad_maximum_fusion
  98.1 1.7 %copy.7 = f32[1,4,4,64,256]{4,2,1,0,3:T(4,128)} copy(f32[1,4,4,64,256]{4,3,2,1,0:T(8,128)S(1)} %pad_maximum_fusion) | data formatting | bytes 2097152 | tf_op jit(solution)/shard_map/concatenate | solution.py:38
  99.7 12.1 %all-to-all-start = ((f32[1,4,4,64,256]{4,2,1,0,3:T(4,128)}), f32[1,4,4,64,256]{4,2,1,0,3:T(4,128)S(1)}, u32[]{:S(2)}, u32[]{:S(2)}) async-start(f32[1,4,4,64,256]{4,2,1,0,3:T(4,128)} %copy.7), calls=%async_computation | async-start | bytes 2097152 | tf_op jit(solution)/shard_map/all_to_all | solution.py:57
  111.9 0.0 copy-done
  111.9 2.0 %sort.17 = (s32[64]{0:T(128)}, s32[64]{0:T(128)S(1)}) sort(s32[64]{0:T(128)S(1)} %dynamic-slice_bitcast_fusion, s32[64]{0:T(128)S(1)} %iota.12), dimensions={0}, to_apply=%region_0.1 | sort | flops 384 | bytes 1024 | tf_op jit(solution)/shard_map/jit(argsort)/sort | solution.py:61
  114.0 26.7 %all-to-all-done = f32[1,4,4,64,256]{4,2,1,0,3:T(4,128)S(1)} async-done(((f32[1,4,4,64,256]{4,2,1,0,3:T(4,128)}), f32[1,4,4,64,256]{4,2,1,0,3:T(4,128)S(1)}, u32[]{:S(2)}, u32[]{:S(2)}) %all-to-all-start) | async-done | bytes 1048608 | tf_op jit(solution)/shard_map/all_to_all | solution.py:57
  140.6 1.2 gather_fusion
  141.8 0.3 broadcast_select_fusion
  142.2 0.2 multiply_add_fusion
  142.5 0.1 multiply_add_fusion.1
  142.8 9.5 %all_to_all.33 = f32[1,4,4,256]{3,1,0,2:T(4,128)S(1)} all-to-all(f32[1,4,4,256]{3,1,0,2:T(4,128)S(1)} %copy.8), channel_id=1, replica_groups=mesh['grp'=4,'tile'=64] {'grp'}, dimensions={2} | all-to-all | bytes 32768 | tf_op jit(solution)/shard_map/all_to_all | solution.py:64
  152.3 0.6 fusion.96
  (30 shorter events, 0.3 us)
Async XLA Ops:
  0.0 111.9 %copy-start = (s32[4,64]{1,0:T(4,128)S(1)}, s32[4,64]{1,0:T(4,128)}, u32[]{:S(2)}) copy-start(s32[4,64]{1,0:T(4,128)} %param.9) | copy-start | bytes 3076
  0.0 1.5 copy-start.2
  0.0 1.5 copy-start.1
  99.7 40.9 %all-to-all-start = ((f32[1,4,4,64,256]{4,2,1,0,3:T(4,128)}), f32[1,4,4,64,256]{4,2,1,0,3:T(4,128)S(1)}, u32[]{:S(2)}, u32[]{:S(2)}) async-start(f32[1,4,4,64,256]{4,2,1,0,3:T(4,128)} %copy.7), calls=%async_computation | async-start | bytes 2097152 | tf_op jit(solution)/shard_map/all_to_all | solution.py:57
where the time goes:
time: 155 us; the launch traced here: 153 us
  matrix products  88.8 us (57%)
  waiting for transfers between devices  26.7 us (17%)
  starting transfers between devices  12.1 us (8%)
  blocking collectives  9.46 us (6%)
  other arithmetic  6.19 us (4%)
  local copies, waits for them, and re-layouts  5.18 us (3%)
  loops' own time  4.23 us (3%)
    dot_general x16, matrix products, shade_cells(): jnp.dot(palette, weights, precision=lax.Precision.HIGHEST, preferred_elem...  88.8 us
    all_to_all x1, waiting for transfers between devices, body(): lax.all_to_all(sectioned, 'tile', split_axis=3, concat_axis=0, tiled=True)  26.7 us
    all_to_all x1, starting transfers between devices, body(): lax.all_to_all(sectioned, 'tile', split_axis=3, concat_axis=0, tiled=True)  12.1 us
    all_to_all x1, blocking collectives, body(): lax.all_to_all(own_group[None], 'grp', split_axis=2, concat_axis=0, tiled...  9.46 us
    another operation x1, loops' own time, render(): colour, transmit = lax.fori_loop(0, depth_count, one_slice, start)  4.23 us
  transfers between devices with their start and end apart: 1, of which 1 were waited for; matrix products, arithmetic and copies ran while one was open for 1% of the time, Pallas kernels for 0%

commit v1 on v0

--- a/solution.py
+++ b/solution.py
@@ -47,6 +47,13 @@
 
 
 def body(bricks, colour_table, opacity_table, depth_order):
+
+    def _link_positions(content):
+        vec_out = jnp.stack(jnp.split(content, jax.lax.axis_size("tile"), axis=3), axis=0)
+        mid_arr = jax.lax.all_to_all(vec_out, "tile", 0, 0)
+        carry_in = jnp.concatenate(mid_arr, axis=0)
+        return carry_in
+
     palette = jnp.concatenate([colour_table, opacity_table[None, :]], axis=0)
     partial_value = render(bricks, palette)
     groups = lax.axis_size("grp")
@@ -54,7 +61,7 @@
     pixels = partial_value.shape[1]
     sub_len = pixels // (groups * members)
     sectioned = partial_value.reshape(1, 4, groups, members, sub_len)
-    layers = lax.all_to_all(sectioned, "tile", split_axis=3, concat_axis=0, tiled=True)
+    layers = _link_positions(sectioned)
     layers = layers.reshape(members, 4, groups, sub_len)
     group_index = lax.axis_index("grp")
     rank_row = lax.dynamic_index_in_dim(depth_order, group_index, 0, keepdims=False)

time: 155 us -> 156 us (level)
    concatenate x2, local copies, waits for them, and re-layouts: 1.74 us -> 0.09 us  [render(): return jnp.concatenate([colour, (1.0 - transmit)[None, :]], axis=0)]
where the time goes in v1:
time: 156 us; the launch traced here: 155 us
  matrix products  88.8 us (57%)
  waiting for transfers between devices  26.7 us (17%)
  starting transfers between devices  12.1 us (8%)
  blocking collectives  9.46 us (6%)
  local copies, waits for them, and re-layouts  6.28 us (4%)
  other arithmetic  6.12 us (4%)
  loops' own time  4.86 us (3%)
    dot_general x16, matrix products, shade_cells(): jnp.dot(palette, weights, precision=lax.Precision.HIGHEST, preferred_elem...  88.8 us
    all_to_all x1, waiting for transfers between devices, _link_positions(): mid_arr = jax.lax.all_to_all(vec_out, 'tile', 0, 0)  26.7 us
    all_to_all x1, starting transfers between devices, _link_positions(): mid_arr = jax.lax.all_to_all(vec_out, 'tile', 0, 0)  12.1 us
    all_to_all x1, blocking collectives, body(): lax.all_to_all(own_group[None], 'grp', split_axis=2, concat_axis=0, tiled...  9.46 us
    another operation x1, loops' own time, render(): colour, transmit = lax.fori_loop(0, depth_count, one_slice, start)  4.86 us
  transfers between devices with their start and end apart: 1, of which 1 were waited for; matrix products, arithmetic and copies ran while one was open for 1% of the time, Pallas kernels for 0%

profile of v1, /device:TPU:8, one launch (start us, length us, event | category | flops | bytes accessed | tf_op | source)
XLA Modules:
  0.0 155.0 jit_solution(2525341883476024231)
XLA Ops:
  0.0 0.0 copy-start
  0.0 0.0 copy-start.2
  0.0 0.0 copy-start.1
  0.0 1.5 copy.136
  1.5 0.0 copy-done.2
  1.5 0.0 copy-done.1
  1.5 96.8 %while.16 = (s32[]{:T(128)}, f32[3,65536]{1,0:T(4,128)S(1)}, f32[65536]{0:T(1024)S(1)}, f32[2,65536]{1,0:T(2,128)S(1)}, f32[4,256]{1,0:T(4,128)S(1)}, /*index=5*...) while((s32[]{:T(128)}, f32[3,65536]{1,0:T(4,128)S(1)}, ...), condition=%wide.region_2.3_spmd.clone, body=%wide.region_1.2_spmd.clone.sunk | while | flops 873332736 | bytes 6062340 | solution.py:37
  1.8 0.6 dynamic-slice_multiply_fusion.9
  2.3 5.4 %fusion.147 = f32[4,65536]{1,0:T(4,128)S(1)} fusion(f32[4,256]{1,0:T(4,128)S(1)} %get-tuple-element.225, f32[8192]{0:T(1024)S(1)} %bitcast.399), kind=kOutput, calls=%fused_computation.16.clone.1 | convolution fusion | flops 109051904 | bytes 167936 | tf_op jit(solution)/shard_map/while/body/eval_jaxpr/dot_general | solution.py:12
  7.8 5.4 %fusion.148 = f32[4,65536]{1,0:T(4,128)S(1)} fusion(f32[4,65536]{1,0:T(4,128)S(1)} %fusion.147, f32[4,256]{1,0:T(4,128)S(1)} %get-tuple-element.225, f32[8192]{0:T(1024)S(1)} %bitcast.398), kind=kOutput, calls=%fused_computation.14.clone.1 | convolution fusion | flops 109051904 | bytes 167936 | tf_op jit(solution)/shard_map/while/body/eval_jaxpr/dot_general | solution.py:12
  13.2 6.0 %fusion.149 = f32[4,65536]{1,0:T(4,128)S(1)} fusion(f32[4,65536]{1,0:T(4,128)S(1)} %fusion.148, f32[4,256]{1,0:T(4,128)S(1)} %get-tuple-element.225, f32[8192]{0:T(1024)S(1)} %bitcast.397), kind=kOutput, calls=%fused_computation.12.clone.1 | convolution fusion | flops 109051904 | bytes 167936 | tf_op jit(solution)/shard_map/while/body/eval_jaxpr/dot_general | solution.py:12
  19.2 5.4 %fusion.150 = f32[4,65536]{1,0:T(4,128)S(1)} fusion(f32[4,65536]{1,0:T(4,128)S(1)} %fusion.149, f32[4,256]{1,0:T(4,128)S(1)} %get-tuple-element.225, f32[8192]{0:T(1024)S(1)} %bitcast.396), kind=kOutput, calls=%fused_computation.10.clone.1 | convolution fusion | flops 109051904 | bytes 167936 | tf_op jit(solution)/shard_map/while/body/eval_jaxpr/dot_general | solution.py:12
  24.6 5.6 %fusion.151 = f32[4,65536]{1,0:T(4,128)S(1)} fusion(f32[4,65536]{1,0:T(4,128)S(1)} %fusion.150, f32[4,256]{1,0:T(4,128)S(1)} %get-tuple-element.225, f32[8192]{0:T(1024)S(1)} %bitcast.395), kind=kOutput, calls=%fused_computation.8.clone.1 | convolution fusion | flops 109051904 | bytes 167936 | tf_op jit(solution)/shard_map/while/body/eval_jaxpr/dot_general | solution.py:12
  30.2 5.4 %fusion.152 = f32[4,65536]{1,0:T(4,128)S(1)} fusion(f32[4,65536]{1,0:T(4,128)S(1)} %fusion.151, f32[4,256]{1,0:T(4,128)S(1)} %get-tuple-element.225, f32[8192]{0:T(1024)S(1)} %bitcast.394), kind=kOutput, calls=%fused_computation.6.clone.1 | convolution fusion | flops 109051904 | bytes 167936 | tf_op jit(solution)/shard_map/while/body/eval_jaxpr/dot_general | solution.py:12
  35.7 5.7 %fusion.153 = f32[4,65536]{1,0:T(4,128)S(1)} fusion(f32[4,65536]{1,0:T(4,128)S(1)} %fusion.152, f32[4,256]{1,0:T(4,128)S(1)} %get-tuple-element.225, f32[8192]{0:T(1024)S(1)} %bitcast.393), kind=kOutput, calls=%fused_computation.4.clone.1 | convolution fusion | flops 109051904 | bytes 167936 | tf_op jit(solution)/shard_map/while/body/eval_jaxpr/dot_general | solution.py:12
  41.3 5.4 %fusion.154 = f32[4,65536]{1,0:T(4,128)S(1)} fusion(f32[4,65536]{1,0:T(4,128)S(1)} %fusion.153, f32[4,256]{1,0:T(4,128)S(1)} %get-tuple-element.225, f32[8192]{0:T(1024)S(1)} %bitcast.392), kind=kOutput, calls=%fused_computation.2.clone.1 | convolution fusion | flops 109051904 | bytes 167936 | tf_op jit(solution)/shard_map/while/body/eval_jaxpr/dot_general | solution.py:12
  46.8 0.3 slice.255
  47.1 0.2 subtract_multiply_fusion.2
  47.2 0.6 fusion.155
  48.3 0.6 dynamic-slice_multiply_fusion.9
  48.8 5.4 %fusion.147 = f32[4,65536]{1,0:T(4,128)S(1)} fusion(f32[4,256]{1,0:T(4,128)S(1)} %get-tuple-element.225, f32[8192]{0:T(1024)S(1)} %bitcast.399), kind=kOutput, calls=%fused_computation.16.clone.1 | convolution fusion | flops 109051904 | bytes 167936 | tf_op jit(solution)/shard_map/while/body/eval_jaxpr/dot_general | solution.py:12
  54.2 5.4 %fusion.148 = f32[4,65536]{1,0:T(4,128)S(1)} fusion(f32[4,65536]{1,0:T(4,128)S(1)} %fusion.147, f32[4,256]{1,0:T(4,128)S(1)} %get-tuple-element.225, f32[8192]{0:T(1024)S(1)} %bitcast.398), kind=kOutput, calls=%fused_computation.14.clone.1 | convolution fusion | flops 109051904 | bytes 167936 | tf_op jit(solution)/shard_map/while/body/eval_jaxpr/dot_general | solution.py:12
  59.7 5.6 %fusion.149 = f32[4,65536]{1,0:T(4,128)S(1)} fusion(f32[4,65536]{1,0:T(4,128)S(1)} %fusion.148, f32[4,256]{1,0:T(4,128)S(1)} %get-tuple-element.225, f32[8192]{0:T(1024)S(1)} %bitcast.397), kind=kOutput, calls=%fused_computation.12.clone.1 | convolution fusion | flops 109051904 | bytes 167936 | tf_op jit(solution)/shard_map/while/body/eval_jaxpr/dot_general | solution.py:12
  65.3 5.4 %fusion.150 = f32[4,65536]{1,0:T(4,128)S(1)} fusion(f32[4,65536]{1,0:T(4,128)S(1)} %fusion.149, f32[4,256]{1,0:T(4,128)S(1)} %get-tuple-element.225, f32[8192]{0:T(1024)S(1)} %bitcast.396), kind=kOutput, calls=%fused_computation.10.clone.1 | convolution fusion | flops 109051904 | bytes 167936 | tf_op jit(solution)/shard_map/while/body/eval_jaxpr/dot_general | solution.py:12
  70.8 5.7 %fusion.151 = f32[4,65536]{1,0:T(4,128)S(1)} fusion(f32[4,65536]{1,0:T(4,128)S(1)} %fusion.150, f32[4,256]{1,0:T(4,128)S(1)} %get-tuple-element.225, f32[8192]{0:T(1024)S(1)} %bitcast.395), kind=kOutput, calls=%fused_computation.8.clone.1 | convolution fusion | flops 109051904 | bytes 167936 | tf_op jit(solution)/shard_map/while/body/eval_jaxpr/dot_general | solution.py:12
  76.4 5.4 %fusion.152 = f32[4,65536]{1,0:T(4,128)S(1)} fusion(f32[4,65536]{1,0:T(4,128)S(1)} %fusion.151, f32[4,256]{1,0:T(4,128)S(1)} %get-tuple-element.225, f32[8192]{0:T(1024)S(1)} %bitcast.394), kind=kOutput, calls=%fused_computation.6.clone.1 | convolution fusion | flops 109051904 | bytes 167936 | tf_op jit(solution)/shard_map/while/body/eval_jaxpr/dot_general | solution.py:12
  81.9 5.8 %fusion.153 = f32[4,65536]{1,0:T(4,128)S(1)} fusion(f32[4,65536]{1,0:T(4,128)S(1)} %fusion.152, f32[4,256]{1,0:T(4,128)S(1)} %get-tuple-element.225, f32[8192]{0:T(1024)S(1)} %bitcast.393), kind=kOutput, calls=%fused_computation.4.clone.1 | convolution fusion | flops 109051904 | bytes 167936 | tf_op jit(solution)/shard_map/while/body/eval_jaxpr/dot_general | solution.py:12
  87.7 5.4 %fusion.154 = f32[4,65536]{1,0:T(4,128)S(1)} fusion(f32[4,65536]{1,0:T(4,128)S(1)} %fusion.153, f32[4,256]{1,0:T(4,128)S(1)} %get-tuple-element.225, f32[8192]{0:T(1024)S(1)} %bitcast.392), kind=kOutput, calls=%fused_computation.2.clone.1 | convolution fusion | flops 109051904 | bytes 167936 | tf_op jit(solution)/shard_map/while/body/eval_jaxpr/dot_general | solution.py:12
  93.1 0.3 slice.255
  93.4 0.2 subtract_multiply_fusion.2
  93.6 0.6 fusion.155
  98.4 0.2 copy.137
  98.5 0.1 constant_dynamic-update-slice_fusion.1
  98.6 0.1 concatenate.20
  100.4 1.3 copy.133
  101.6 12.1 %all-to-all-start = ((f32[64,1,4,4,1,256]{5,3,2,4,1,0:T(4,128)}), f32[64,1,4,4,1,256]{5,3,2,4,1,0:T(4,128)S(1)}, u32[]{:S(2)}, u32[]{:S(2)}) async-start(f32[64,1,4,4,1,256]{5,3,2,4,1,0:T(4,128)} %copy.133), calls=%async_computation | async-start | bytes 2097152 | tf_op jit(solution)/shard_map/all_to_all | solution.py:53
  113.8 0.0 copy-done
  113.8 2.0 %sort.17 = (s32[64]{0:T(128)}, s32[64]{0:T(128)S(1)}) sort(s32[64]{0:T(128)S(1)} %dynamic-slice_bitcast_fusion, s32[64]{0:T(128)S(1)} %iota.12), dimensions={0}, to_apply=%region_0.1 | sort | flops 384 | bytes 1024 | tf_op jit(solution)/shard_map/jit(argsort)/sort | solution.py:68
  115.9 26.7 %all-to-all-done = f32[64,1,4,4,1,256]{5,3,2,4,1,0:T(4,128)S(1)} async-done(((f32[64,1,4,4,1,256]{5,3,2,4,1,0:T(4,128)}), f32[64,1,4,4,1,256]{5,3,2,4,1,0:T(4,128)S(1)}, u32[]{:S(2)}, u32[]{:S(2)}) %all-to-all-start) | async-done | bytes 1048608 | tf_op jit(solution)/shard_map/all_to_all | solution.py:53
  142.5 1.2 gather_fusion
  143.7 0.3 broadcast_select_fusion
  144.1 0.2 multiply_add_fusion
  144.4 0.1 multiply_add_fusion.1
  144.7 9.5 %all_to_all.23 = f32[1,4,4,256]{3,1,0,2:T(4,128)S(1)} all-to-all(f32[1,4,4,256]{3,1,0,2:T(4,128)S(1)} %copy.134), channel_id=1, replica_groups=mesh['grp'=4,'tile'=64] {'grp'}, dimensions={2} | all-to-all | bytes 32768 | tf_op jit(solution)/shard_map/all_to_all | solution.py:71
  154.2 0.6 fusion.96
  (95 shorter events, 1.8 us)
Async XLA Ops:
  0.0 113.8 %copy-start = (s32[4,64]{1,0:T(4,128)S(1)}, s32[4,64]{1,0:T(4,128)}, u32[]{:S(2)}) copy-start(s32[4,64]{1,0:T(4,128)} %param.9) | copy-start | bytes 3076
  0.0 1.5 copy-start.2
  0.0 1.5 copy-start.1
  101.6 40.9 %all-to-all-start = ((f32[64,1,4,4,1,256]{5,3,2,4,1,0:T(4,128)}), f32[64,1,4,4,1,256]{5,3,2,4,1,0:T(4,128)S(1)}, u32[]{:S(2)}, u32[]{:S(2)}) async-start(f32[64,1,4,4,1,256]{5,3,2,4,1,0:T(4,128)} %copy.133), calls=%async_computation | async-start | bytes 2097152 | tf_op jit(solution)/shard_map/all_to_all | solution.py:53
